TPU v7x, 32 devices: a whole 2x2x4 slice. The times are simulated.
32 devices in a mesh: grp: 8 (over z, core), dev: 4 (over y, x).
Axes of the slice: x: 2, y: 2, z: 4, core: 2. Of those that a mesh axis runs over, the one named last changes fastest.
Arguments:
- tokens: bfloat16 [4096, 2304], P(('grp', 'dev')), may hold values from -6 to 6
- cotangent: bfloat16 [4096, 2304], P(('grp', 'dev')), may hold values from -6 to 6
- expert_ids: int32 [4096, 8], P(('grp', 'dev')), may hold values from 0 to 31, as said below
- combine_weights: bfloat16 [4096, 8], P(('grp', 'dev')), may hold values from 0.099609375 to 0.3984375
- live_counts: int32 [32, 2], P(('grp', 'dev')), may hold values from 32 to 64, as said below
- gate_weight: bfloat16 [32, 2304, 512], P(('grp', 'dev')), may hold values from -0.125 to 0.125
- up_weight: bfloat16 [32, 2304, 512], P(('grp', 'dev')), may hold values from -0.125 to 0.125
- down_weight: bfloat16 [32, 512, 2304], P(('grp', 'dev')), may hold values from -0.25 to 0.25
Outputs:
- mixed_out: bfloat16 [4096, 2304], P(('grp', 'dev'))
- input_grad: bfloat16 [4096, 2304], P(('grp', 'dev'))
Inputs may be any that keep to these rules, and one draw needn't show every extreme that they name: `expert_ids`: expert g * 4 + l is expert l of group g. Each row names 8 distinct experts lying in 4 distinct groups, 2 in each, and entries 2 q to 2 q + 1 share one group. Counting all 64 rows of one device's micro-batch, live or not, each expert is named by exactly 16 rows and each group by exactly 32 rows; so at most 16 live rows name one expert, exactly 16 in a full micro-batch. The first live_counts[d, m] rows of device d's micro-batch m are live, the others are padding; some micro-batch of some device is full.
All inputs are finite; a program needn't handle non-finite values.
Results may differ from a plain program's by a relative error of at most 0.0085.
Values may be sent and summed in bfloat16 or wider, within the bound.
A program may use at most 128 MiB of HBM per device.

v0:
```python
import jax
import jax.numpy as jnp
from jax import lax
from jax.sharding import PartitionSpec as P

PAIR = 2


def expert_pass(rows_x, rows_dy, gate_matrix, up_matrix, down_matrix):
    contract = (((1,), (1,)), ((), ()))
    gate_pre = jnp.dot(rows_x, gate_matrix, preferred_element_type=jnp.float32)
    up_pre = jnp.dot(rows_x, up_matrix, preferred_element_type=jnp.float32)
    sigmoid_gate = jax.nn.sigmoid(gate_pre)
    gate_act = gate_pre * sigmoid_gate
    hidden = (gate_act * up_pre).astype(jnp.bfloat16)
    out_rows = jnp.dot(hidden, down_matrix, preferred_element_type=jnp.float32).astype(jnp.bfloat16)
    hidden_grad = lax.dot_general(
        rows_dy, down_matrix, contract, preferred_element_type=jnp.float32
    )
    gate_grad = (
        hidden_grad * up_pre * sigmoid_gate * (1.0 + gate_pre * (1.0 - sigmoid_gate))
    ).astype(jnp.bfloat16)
    up_grad = (hidden_grad * gate_act).astype(jnp.bfloat16)
    grad_rows = lax.dot_general(
        gate_grad, gate_matrix, contract, preferred_element_type=jnp.float32
    )
    grad_rows = grad_rows + lax.dot_general(
        up_grad, up_matrix, contract, preferred_element_type=jnp.float32
    )
    return (out_rows, grad_rows.astype(jnp.bfloat16))


def apply_blocks(piece_tokens, piece_cotan, matrices, model_width):
    dims_shape = piece_tokens.shape
    out_rows, grad_rows = expert_pass(
        piece_tokens.reshape(-1, model_width),
        piece_cotan.reshape(-1, model_width),
        matrices[0],
        matrices[1],
        matrices[2],
    )
    return (out_rows.reshape(dims_shape), grad_rows.reshape(dims_shape))


def earlier_counts(member):
    return jnp.cumsum(member, axis=1) - member


def take_rows(table, indices):
    return table[indices]


def micro_run(tokens_m, cotan_m, ids_m, weights_m, alive_m, matrices, groups, group_size, capacity):
    count_mb, rows_mb, model_width = tokens_m.shape
    top_count = ids_m.shape[2]
    picked_groups = top_count // PAIR
    experts = groups * group_size
    mb_index = jnp.arange(count_mb, dtype=jnp.int32)[:, None, None]
    alive_int = alive_m.astype(jnp.int32)
    member = (
        jnp.sum(
            (ids_m[..., None] == jnp.arange(experts, dtype=jnp.int32)).astype(jnp.int32), axis=2
        )
        * alive_int[..., None]
    )
    slot_index = jnp.take_along_axis(earlier_counts(member), ids_m, axis=2)
    flat_tokens = tokens_m.reshape(count_mb * rows_mb, model_width)
    flat_cotan = cotan_m.reshape(count_mb * rows_mb, model_width)
    pair_ids = ids_m.reshape(count_mb, rows_mb, picked_groups, PAIR)
    group_of = pair_ids[..., 0] // group_size
    group_member = (
        jnp.sum(
            (group_of[..., None] == jnp.arange(groups, dtype=jnp.int32)).astype(jnp.int32), axis=2
        )
        * alive_int[..., None]
    )
    group_slot = jnp.take_along_axis(earlier_counts(group_member), group_of, axis=2)
    group_cap = group_size * capacity // PAIR
    group_row = (group_of * count_mb + mb_index) * group_cap + group_slot
    group_total = groups * count_mb * group_cap
    group_picker = (group_row[..., None] == jnp.arange(group_total, dtype=jnp.int32)).astype(
        jnp.int32
    ) * alive_int[..., None, None]
    token_map = (
        jnp.sum(group_picker, axis=2).astype(jnp.bfloat16).reshape(count_mb * rows_mb, group_total)
    )
    send_tokens = jnp.einsum(
        "sr,sd->rd", token_map, flat_tokens, preferred_element_type=jnp.float32
    ).astype(jnp.bfloat16)
    send_cotan = jnp.einsum(
        "sr,sd->rd", token_map, flat_cotan, preferred_element_type=jnp.float32
    ).astype(jnp.bfloat16)
    send_tokens = send_tokens.reshape(groups, count_mb, group_cap, model_width)
    send_cotan = send_cotan.reshape(groups, count_mb, group_cap, model_width)
    target = pair_ids % group_size * capacity + slot_index.reshape(
        count_mb, rows_mb, picked_groups, PAIR
    )
    row_target = jnp.einsum("mbqr,mbqp->rp", group_picker, target + 1) - 1
    row_target = row_target.reshape(groups, count_mb, group_cap, PAIR)
    pair_weights = weights_m.reshape(count_mb, rows_mb, picked_groups, PAIR).astype(jnp.float32)
    row_weight = jnp.einsum(
        "mbqr,mbqp->rp",
        group_picker.astype(jnp.float32),
        pair_weights,
        precision=lax.Precision.HIGHEST,
    )
    row_weight = row_weight.astype(jnp.bfloat16).reshape(groups, count_mb, group_cap, PAIR)
    received = (
        lax.all_to_all(send_tokens, "grp", split_axis=0, concat_axis=0, tiled=True),
        lax.all_to_all(send_cotan, "grp", split_axis=0, concat_axis=0, tiled=True),
        lax.all_to_all(row_weight, "grp", split_axis=0, concat_axis=0, tiled=True),
        lax.all_to_all(row_target, "grp", split_axis=0, concat_axis=0, tiled=True),
    )
    in_tokens, in_cotan, in_weight, in_target = received
    blocks = groups * count_mb
    slots_group = group_size * capacity
    select = (
        in_target.reshape(blocks, group_cap, PAIR, 1) == jnp.arange(slots_group, dtype=jnp.int32)
    ).astype(jnp.int32)
    select = jnp.sum(select, axis=2).astype(jnp.bfloat16)
    place_tokens = jnp.einsum(
        "bjv,bjd->bvd",
        select,
        in_tokens.reshape(blocks, group_cap, model_width),
        preferred_element_type=jnp.float32,
    )
    place_cotan = jnp.einsum(
        "bjv,bjd->bvd",
        select,
        in_cotan.reshape(blocks, group_cap, model_width),
        preferred_element_type=jnp.float32,
    )
    place_tokens = place_tokens.astype(jnp.bfloat16).reshape(
        groups, count_mb, group_size, capacity * model_width
    )
    place_cotan = place_cotan.astype(jnp.bfloat16).reshape(
        groups, count_mb, group_size, capacity * model_width
    )
    results = apply_blocks(
        lax.all_to_all(place_tokens, "dev", split_axis=2, concat_axis=2, tiled=True),
        lax.all_to_all(place_cotan, "dev", split_axis=2, concat_axis=2, tiled=True),
        matrices,
        model_width,
    )
    back_out = lax.all_to_all(results[0], "dev", split_axis=2, concat_axis=2, tiled=True)
    back_grad = lax.all_to_all(results[1], "dev", split_axis=2, concat_axis=2, tiled=True)
    row_index = jnp.maximum(in_target, 0).reshape(blocks, group_cap * PAIR)
    picked_out = jax.vmap(take_rows)(back_out.reshape(blocks, slots_group, model_width), row_index)
    picked_grad = jax.vmap(take_rows)(
        back_grad.reshape(blocks, slots_group, model_width), row_index
    )
    picked_out = picked_out.reshape(groups, count_mb, group_cap, PAIR * model_width)
    picked_grad = picked_grad.reshape(groups, count_mb, group_cap, PAIR * model_width)
    weight_rows = in_weight.astype(jnp.float32)
    pair_out = jnp.zeros((groups, count_mb, group_cap, model_width), jnp.float32)
    pair_grad = jnp.zeros((groups, count_mb, group_cap, model_width), jnp.float32)
    for pair_slot in range(PAIR):
        lower = pair_slot * model_width
        upper = lower + model_width
        factor = weight_rows[..., pair_slot : pair_slot + 1]
        pair_out = pair_out + factor * picked_out[..., lower:upper].astype(jnp.float32)
        pair_grad = pair_grad + factor * picked_grad[..., lower:upper].astype(jnp.float32)
    pair_out = pair_out.astype(jnp.bfloat16)
    pair_grad = pair_grad.astype(jnp.bfloat16)
    ret_out, ret_grad = (
        lax.all_to_all(pair_out, "grp", split_axis=0, concat_axis=0, tiled=True),
        lax.all_to_all(pair_grad, "grp", split_axis=0, concat_axis=0, tiled=True),
    )
    group_rows_flat = group_row.reshape(count_mb, rows_mb * picked_groups)
    gathered_out = ret_out.reshape(group_total, model_width)[group_rows_flat].reshape(
        count_mb, rows_mb, picked_groups * model_width
    )
    gathered_grad = ret_grad.reshape(group_total, model_width)[group_rows_flat].reshape(
        count_mb, rows_mb, picked_groups * model_width
    )
    sum_out = jnp.zeros((count_mb, rows_mb, model_width), jnp.float32)
    sum_grad = jnp.zeros((count_mb, rows_mb, model_width), jnp.float32)
    for group_slot in range(picked_groups):
        lower = group_slot * model_width
        upper = lower + model_width
        sum_out = sum_out + gathered_out[..., lower:upper].astype(jnp.float32)
        sum_grad = sum_grad + gathered_grad[..., lower:upper].astype(jnp.float32)
    mixed_part = jnp.where(alive_m[..., None], sum_out, 0.0).astype(jnp.bfloat16)
    grad_part = jnp.where(alive_m[..., None], sum_grad, 0.0).astype(jnp.bfloat16)
    return (mixed_part, grad_part)


def local(
    tokens, cotangent, expert_ids, combine_weights, live_counts, gate_weight, up_weight, down_weight
):
    groups = lax.axis_size("grp")
    group_size = lax.axis_size("dev")
    experts = groups * group_size
    micro_count = live_counts.shape[1]
    rows_mb = tokens.shape[0] // micro_count
    model_width = tokens.shape[1]
    top_count = expert_ids.shape[1]
    capacity = top_count * rows_mb // experts
    matrices = (gate_weight[0], up_weight[0], down_weight[0])
    alive_all = jnp.arange(rows_mb, dtype=jnp.int32)[None, :] < live_counts[0][:, None]
    tokens_all = tokens.reshape(micro_count, rows_mb, model_width)
    cotan_all = cotangent.reshape(micro_count, rows_mb, model_width)
    ids_all = expert_ids.reshape(micro_count, rows_mb, top_count)
    weights_all = combine_weights.reshape(micro_count, rows_mb, top_count)
    mixed_list = []
    grad_list = []
    for micro_index in range(micro_count):
        upper = micro_index + 1
        mixed_part, grad_part = micro_run(
            tokens_all[micro_index:upper],
            cotan_all[micro_index:upper],
            ids_all[micro_index:upper],
            weights_all[micro_index:upper],
            alive_all[micro_index:upper],
            matrices,
            groups,
            group_size,
            capacity,
        )
        mixed_list.append(mixed_part)
        grad_list.append(grad_part)
    mixed_out = jnp.concatenate(mixed_list, axis=0)
    input_grad = jnp.concatenate(grad_list, axis=0)
    return (
        mixed_out.reshape(micro_count * rows_mb, model_width),
        input_grad.reshape(micro_count * rows_mb, model_width),
    )


def solution(mesh):
    in_specs = (
        P(("grp", "dev"), None),
        P(("grp", "dev"), None),
        P(("grp", "dev"), None),
        P(("grp", "dev"), None),
        P(("grp", "dev"), None),
        P(("grp", "dev"), None, None),
        P(("grp", "dev"), None, None),
        P(("grp", "dev"), None, None),
    )
    out_specs = (P(("grp", "dev"), None), P(("grp", "dev"), None))
    return jax.shard_map(local, mesh=mesh, in_specs=in_specs, out_specs=out_specs, check_vma=False)
```

profile of v0, /device:TPU:1, one launch (start us, length us, event | category | flops | bytes accessed | tf_op | source)
XLA Modules:
  0.0 649.1 jit_solution(983745397550774359)
XLA Ops:
  6.8 6.4 all-to-all-start
  26.5 5.1 all-to-all-start.6
  41.2 4.1 all-to-all-done.1
  54.2 4.2 all-to-all-start.2
  60.9 25.9 %all-to-all-done.2 = bf16[8,1,32,2304]{3,2,1,0:T(8,128)(2,1)S(1)} async-done(((bf16[8,1,32,2304]{3,2,1,0:T(8,128)(2,1)}), bf16[8,1,32,2304]{3,2,1,0:T(8,128)(2,1)S(1)}, u32[]{:S(2)}, u32[]{:S(2)}) %all-to-all-start.2) | async-done | bytes 1179680 | tf_op jit(solution)/shard_map/all_to_all | solution.py:109
  87.8 4.4 all-to-all-start.12
  96.1 24.5 %all-to-all-done.12 = bf16[8,1,32,2304]{3,2,1,0:T(8,128)(2,1)S(1)} async-done(((bf16[8,1,32,2304]{3,2,1,0:T(8,128)(2,1)}), bf16[8,1,32,2304]{3,2,1,0:T(8,128)(2,1)S(1)}, u32[]{:S(2)}, u32[]{:S(2)}) %all-to-all-start.12) | async-done | bytes 1179680 | tf_op jit(solution)/shard_map/all_to_all | solution.py:110
  121.8 4.4 all-to-all-start.8
  128.7 25.9 %all-to-all-done.8 = bf16[8,1,32,2304]{3,2,1,0:T(8,128)(2,1)S(1)} async-done(((bf16[8,1,32,2304]{3,2,1,0:T(8,128)(2,1)}), bf16[8,1,32,2304]{3,2,1,0:T(8,128)(2,1)S(1)}, u32[]{:S(2)}, u32[]{:S(2)}) %all-to-all-start.8) | async-done | bytes 1179680 | tf_op jit(solution)/shard_map/all_to_all | solution.py:109
  155.7 4.4 all-to-all-start.16
  165.2 4.7 reshape.1069
  169.9 4.4 copy.221
  174.3 14.3 %all-to-all-done.16 = bf16[8,1,32,2304]{3,2,1,0:T(8,128)(2,1)S(1)} async-done(((bf16[8,1,32,2304]{3,2,1,0:T(8,128)(2,1)}), bf16[8,1,32,2304]{3,2,1,0:T(8,128)(2,1)S(1)}, u32[]{:S(2)}, u32[]{:S(2)}) %all-to-all-start.16) | async-done | bytes 1179680 | tf_op jit(solution)/shard_map/all_to_all | solution.py:110
  188.6 4.7 all-to-all-start.3
  196.9 4.7 reshape.1098
  201.6 4.3 copy.251
  206.0 14.6 %all-to-all-done.3 = bf16[8,1,4,36864]{3,0,1,2:T(8,128)(2,1)} async-done(((bf16[8,1,4,36864]{3,0,1,2:T(8,128)(2,1)}), bf16[8,1,4,36864]{3,0,1,2:T(8,128)(2,1)}, u32[]{:S(2)}, u32[]{:S(2)}) %all-to-all-start.3) | async-done | bytes 2359328 | tf_op jit(solution)/shard_map/all_to_all | solution.py:140
  220.6 4.5 all-to-all-start.13
  229.5 4.7 reshape.1086
  234.2 4.4 copy.240
  238.6 13.8 %all-to-all-done.13 = bf16[8,1,4,36864]{3,0,1,2:T(8,128)(2,1)} async-done(((bf16[8,1,4,36864]{3,0,1,2:T(8,128)(2,1)}), bf16[8,1,4,36864]{3,0,1,2:T(8,128)(2,1)}, u32[]{:S(2)}, u32[]{:S(2)}) %all-to-all-start.13) | async-done | bytes 2359328 | tf_op jit(solution)/shard_map/all_to_all | solution.py:141
  252.4 4.5 all-to-all-start.9
  260.0 4.7 reshape.1107
  264.7 4.3 copy.258
  269.0 4.9 copy.222
  274.0 4.7 reshape.1070
  284.2 5.0 all-to-all-start.17
  289.2 4.7 fusion.12
  293.9 4.9 copy.252
  298.8 4.8 reshape.1099
  312.4 4.7 reshape.1100
  317.1 4.4 copy.253
  321.5 4.5 all-to-all-start.14
  326.0 5.0 convolution_convert_fusion.4
  331.0 4.7 reshape.1071
  335.7 4.4 copy.223
  340.1 4.9 copy.241
  345.0 4.7 reshape.1087
  353.2 4.7 all-to-all-start.4
  357.9 4.8 fusion.10
  362.7 4.9 copy.259
  367.6 4.8 reshape.1108
  390.9 5.0 convolution_convert_fusion.2
  395.9 4.7 reshape.1088
  400.6 4.3 copy.242
  404.9 13.1 %all-to-all-done.18 = bf16[8,1,4,36864]{3,0,1,2:T(8,128)(2,1)S(1)} async-done(((bf16[8,1,4,36864]{3,0,1,2:T(8,128)(2,1)}), bf16[8,1,4,36864]{3,0,1,2:T(8,128)(2,1)S(1)}, u32[]{:S(2)}, u32[]{:S(2)}) %all-to-all-start.18) | async-done | bytes 2359328 | tf_op jit(solution)/shard_map/all_to_all | solution.py:146
  419.5 4.7 all-to-all-start.10
  425.1 4.9 copy.254
  433.7 12.2 %gather_fusion.6 = bf16[512,2304]{1,0:T(8,128)(2,1)} fusion(bf16[8,64,2304]{2,1,0:T(8,128)(2,1)S(1)} %reshape.1101, s32[512]{0:T(512)S(1)} %reshape.1181), kind=kCustom, calls=%fused_computation.10 | custom fusion | bytes 4722688 | tf_op jit(solution)/shard_map/vmap()/gather | solution.py:50
  445.9 4.2 reshape.1102
  450.1 4.9 copy.224
  458.6 12.2 %gather_fusion.4 = bf16[512,2304]{1,0:T(8,128)(2,1)} fusion(bf16[8,64,2304]{2,1,0:T(8,128)(2,1)S(1)} %reshape.1072, s32[512]{0:T(512)S(1)} %reshape.1181), kind=kCustom, calls=%fused_computation.8 | custom fusion | bytes 4722688 | tf_op jit(solution)/shard_map/vmap()/gather | solution.py:50
  470.9 4.3 reshape.1074
  479.0 33.2 %all_to_all.100 = bf16[8,1,32,2304]{3,2,1,0:T(8,128)(2,1)} all-to-all(bf16[8,1,32,2304]{3,2,1,0:T(8,128)(2,1)S(1)} %get-tuple-element.4), channel_id=1, replica_groups=mesh['grp'=8,'dev'=4] {'grp'}, dimensions={0} | all-to-all | bytes 2359296 | tf_op jit(solution)/shard_map/all_to_all | solution.py:167
  512.2 4.8 all-to-all-start.5
  528.7 12.2 %gather_fusion.7 = bf16[512,2304]{1,0:T(8,128)(2,1)} fusion(bf16[8,64,2304]{2,1,0:T(8,128)(2,1)S(1)} %reshape.1110, s32[512]{0:T(512)S(1)} %reshape.1187), kind=kCustom, calls=%fused_computation.11 | custom fusion | bytes 4722688 | tf_op jit(solution)/shard_map/vmap()/gather | solution.py:50
  540.9 4.2 reshape.1111
  545.1 4.9 copy.243
  553.6 12.3 %gather_fusion.5 = bf16[512,2304]{1,0:T(8,128)(2,1)} fusion(bf16[8,64,2304]{2,1,0:T(8,128)(2,1)S(1)} %reshape.1089, s32[512]{0:T(512)S(1)} %reshape.1187), kind=kCustom, calls=%fused_computation.9 | custom fusion | bytes 4722688 | tf_op jit(solution)/shard_map/vmap()/gather | solution.py:50
  565.9 4.3 reshape.1091
  570.2 4.1 add_convert_fusion
  574.4 33.9 %all_to_all.101 = bf16[8,1,32,2304]{3,2,1,0:T(8,128)(2,1)} all-to-all(bf16[8,1,32,2304]{3,2,1,0:T(8,128)(2,1)} %get-tuple-element.7), channel_id=1, replica_groups=mesh['grp'=8,'dev'=4] {'grp'}, dimensions={0} | all-to-all | bytes 2359296 | tf_op jit(solution)/shard_map/all_to_all | solution.py:166
  608.3 4.5 all-to-all-start.19
  629.9 11.3 %all-to-all-done.19 = bf16[8,1,32,2304]{3,2,1,0:T(8,128)(2,1)S(1)} async-done(((bf16[8,1,32,2304]{3,2,1,0:T(8,128)(2,1)}), bf16[8,1,32,2304]{3,2,1,0:T(8,128)(2,1)S(1)}, u32[]{:S(2)}, u32[]{:S(2)}) %all-to-all-start.19) | async-done | bytes 1179680 | tf_op jit(solution)/shard_map/all_to_all | solution.py:167
  (205 shorter events, 155.4 us)
Async XLA Ops:
  0.6 278.1 %copy-start = (bf16[1,2304,512]{2,1,0:T(8,128)(2,1)S(1)}, bf16[1,2304,512]{2,1,0:T(8,128)(2,1)}, u32[]{:S(2)}) copy-start(bf16[1,2304,512]{2,1,0:T(8,128)(2,1)} %param.17) | copy-start | bytes 7077892
  2.1 29.5 %copy-start.22 = (s32[64]{0:T(128)}, s32[64]{0:T(128)S(1)}, u32[]{:S(2)}) copy-start(s32[64]{0:T(128)S(1)} %get-tuple-element.29) | copy-start | bytes 772
  3.5 2.2 copy-start.30
  3.6 9.7 %copy-start.19 = (s32[128,8]{0,1:T(8,128)S(1)}, s32[128,8]{0,1:T(8,128)}, u32[]{:S(2)}) copy-start(s32[128,8]{0,1:T(8,128)} %param.14) | copy-start | bytes 12292
  5.7 34.6 %copy-start.23 = (s32[1,64,4]{1,2,0:T(4,128)}, s32[1,64,4]{1,2,0:T(4,128)S(1)}, u32[]{:S(2)}) copy-start(s32[1,64,4]{1,2,0:T(4,128)S(1)} %select_add_fusion.1) | copy-start | bytes 3076
  6.8 19.7 %all-to-all-start = ((bf16[8,1,32,2]{2,3,1,0:T(2,128)(2,1)}), bf16[8,1,32,2]{2,3,1,0:T(2,128)(2,1)S(1)}, u32[]{:S(2)}, u32[]{:S(2)}) async-start(bf16[8,1,32,2]{2,3,1,0:T(2,128)(2,1)} %copy.215), calls=%async_computation | async-start | bytes 8192 | tf_op jit(solution)/shard_map/all_to_all | solution.py:111
  22.8 26.4 %copy-start.18 = (bf16[128,2304]{1,0:T(8,128)(2,1)S(1)}, bf16[128,2304]{1,0:T(8,128)(2,1)}, u32[]{:S(2)}) copy-start(bf16[128,2304]{1,0:T(8,128)(2,1)} %param.12) | copy-start | bytes 1769476
  25.0 11.4 %copy-start.25 = (s32[1,64,4]{1,2,0:T(4,128)}, s32[1,64,4]{1,2,0:T(4,128)S(1)}, u32[]{:S(2)}) copy-start(s32[1,64,4]{1,2,0:T(4,128)S(1)} %select_add_fusion) | copy-start | bytes 3076
  26.5 9.9 %all-to-all-start.6 = ((bf16[8,1,32,2]{2,3,1,0:T(2,128)(2,1)}), bf16[8,1,32,2]{2,3,1,0:T(2,128)(2,1)S(1)}, u32[]{:S(2)}, u32[]{:S(2)}) async-start(bf16[8,1,32,2]{2,3,1,0:T(2,128)(2,1)} %copy.234), calls=%async_computation.6 | async-start | bytes 8192 | tf_op jit(solution)/shard_map/all_to_all | solution.py:111
  36.4 8.9 %all-to-all-start.1 = ((s32[8,1,32,2]{2,3,1,0:T(2,128)}), s32[8,1,32,2]{2,3,1,0:T(2,128)S(1)}, u32[]{:S(2)}, u32[]{:S(2)}) async-start(s32[8,1,32,2]{2,3,1,0:T(2,128)} %copy.219), calls=%async_computation.1 | async-start | bytes 16384 | tf_op jit(solution)/shard_map/all_to_all | solution.py:112
  40.5 13.7 %copy-start.16 = (s32[64,256]{1,0:T(8,128)}, s32[64,256]{1,0:T(8,128)S(1)}, u32[]{:S(2)}) copy-start(s32[64,256]{1,0:T(8,128)S(1)} %select_reduce_fusion.1) | copy-start | bytes 196612
  45.3 8.9 %copy-start.20 = (s32[8,1,32,2]{2,3,1,0:T(2,128)}, s32[8,1,32,2]{2,3,1,0:T(2,128)S(1)}, u32[]{:S(2)}) copy-start(s32[8,1,32,2]{2,3,1,0:T(2,128)S(1)} %all-to-all-done.1) | copy-start | bytes 6148
  45.3 8.9 %all-to-all-start.7 = ((s32[8,1,32,2]{2,3,1,0:T(2,128)}), s32[8,1,32,2]{2,3,1,0:T(2,128)S(1)}, u32[]{:S(2)}, u32[]{:S(2)}) async-start(s32[8,1,32,2]{2,3,1,0:T(2,128)} %copy.238), calls=%async_computation.7 | async-start | bytes 16384 | tf_op jit(solution)/shard_map/all_to_all | solution.py:112
  54.2 32.6 %all-to-all-start.2 = ((bf16[8,1,32,2304]{3,2,1,0:T(8,128)(2,1)}), bf16[8,1,32,2304]{3,2,1,0:T(8,128)(2,1)S(1)}, u32[]{:S(2)}, u32[]{:S(2)}) async-start(bf16[8,1,32,2304]{3,2,1,0:T(8,128)(2,1)} %bitcast.212), calls=%async_computation.2 | async-start | bytes 2359296 | tf_op jit(solution)/shard_map/all_to_all | solution.py:109
  86.8 1.0 copy-start.12
  87.8 32.9 %all-to-all-start.12 = ((bf16[8,1,32,2304]{3,2,1,0:T(8,128)(2,1)}), bf16[8,1,32,2304]{3,2,1,0:T(8,128)(2,1)S(1)}, u32[]{:S(2)}, u32[]{:S(2)}) async-start(bf16[8,1,32,2304]{3,2,1,0:T(8,128)(2,1)} %bitcast.211), calls=%async_computation.12 | async-start | bytes 2359296 | tf_op jit(solution)/shard_map/all_to_all | solution.py:110
  93.0 0.6 copy-start.17
  120.6 1.1 copy-start.11
  121.8 32.9 %all-to-all-start.8 = ((bf16[8,1,32,2304]{3,2,1,0:T(8,128)(2,1)}), bf16[8,1,32,2304]{3,2,1,0:T(8,128)(2,1)S(1)}, u32[]{:S(2)}, u32[]{:S(2)}) async-start(bf16[8,1,32,2304]{3,2,1,0:T(8,128)(2,1)} %bitcast.213), calls=%async_computation.8 | async-start | bytes 2359296 | tf_op jit(solution)/shard_map/all_to_all | solution.py:109
  154.6 1.1 copy-start.10
  155.7 32.9 %all-to-all-start.16 = ((bf16[8,1,32,2304]{3,2,1,0:T(8,128)(2,1)}), bf16[8,1,32,2304]{3,2,1,0:T(8,128)(2,1)S(1)}, u32[]{:S(2)}, u32[]{:S(2)}) async-start(bf16[8,1,32,2304]{3,2,1,0:T(8,128)(2,1)} %bitcast.210), calls=%async_computation.16 | async-start | bytes 2359296 | tf_op jit(solution)/shard_map/all_to_all | solution.py:110
  161.0 0.7 copy-start.14
  188.6 32.0 %all-to-all-start.3 = ((bf16[8,1,4,36864]{3,0,1,2:T(8,128)(2,1)}), bf16[8,1,4,36864]{3,0,1,2:T(8,128)(2,1)}, u32[]{:S(2)}, u32[]{:S(2)}) async-start(bf16[8,1,4,36864]{3,0,1,2:T(8,128)(2,1)} %copy.221), calls=%async_computation.3 | async-start | bytes 4718592 | tf_op jit(solution)/shard_map/all_to_all | solution.py:140
  220.6 31.8 %all-to-all-start.13 = ((bf16[8,1,4,36864]{3,0,1,2:T(8,128)(2,1)}), bf16[8,1,4,36864]{3,0,1,2:T(8,128)(2,1)}, u32[]{:S(2)}, u32[]{:S(2)}) async-start(bf16[8,1,4,36864]{3,0,1,2:T(8,128)(2,1)} %copy.251), calls=%async_computation.13 | async-start | bytes 4718592 | tf_op jit(solution)/shard_map/all_to_all | solution.py:141
  225.3 0.7 copy-start.15
  252.4 31.7 %all-to-all-start.9 = ((bf16[8,1,4,36864]{3,0,1,2:T(8,128)(2,1)}), bf16[8,1,4,36864]{3,0,1,2:T(8,128)(2,1)}, u32[]{:S(2)}, u32[]{:S(2)}) async-start(bf16[8,1,4,36864]{3,0,1,2:T(8,128)(2,1)} %copy.240), calls=%async_computation.9 | async-start | bytes 4718592 | tf_op jit(solution)/shard_map/all_to_all | solution.py:140
  284.2 37.3 %all-to-all-start.17 = ((bf16[8,1,4,36864]{3,0,1,2:T(8,128)(2,1)}), bf16[8,1,4,36864]{3,0,1,2:T(8,128)(2,1)}, u32[]{:S(2)}, u32[]{:S(2)}) async-start(bf16[8,1,4,36864]{3,0,1,2:T(8,128)(2,1)} %copy.258), calls=%async_computation.17 | async-start | bytes 4718592 | tf_op jit(solution)/shard_map/all_to_all | solution.py:141
  303.6 3.9 copy-start.33
  307.5 1.8 copy-start.8
  321.5 31.8 %all-to-all-start.14 = ((bf16[8,1,4,36864]{3,0,1,2:T(8,128)(2,1)}), bf16[8,1,4,36864]{3,0,1,2:T(8,128)(2,1)}, u32[]{:S(2)}, u32[]{:S(2)}) async-start(bf16[8,1,4,36864]{3,0,1,2:T(8,128)(2,1)} %copy.253), calls=%async_computation.14 | async-start | bytes 4718592 | tf_op jit(solution)/shard_map/all_to_all | solution.py:146
  353.2 34.0 %all-to-all-start.4 = ((bf16[8,1,4,36864]{3,0,1,2:T(8,128)(2,1)}), bf16[8,1,4,36864]{3,0,1,2:T(8,128)(2,1)}, u32[]{:S(2)}, u32[]{:S(2)}) async-start(bf16[8,1,4,36864]{3,0,1,2:T(8,128)(2,1)} %copy.223), calls=%async_computation.4 | async-start | bytes 4718592 | tf_op jit(solution)/shard_map/all_to_all | solution.py:145
  372.3 3.9 copy-start.34
  376.2 1.8 copy-start.9
  387.3 30.8 %all-to-all-start.18 = ((bf16[8,1,4,36864]{3,0,1,2:T(8,128)(2,1)}), bf16[8,1,4,36864]{3,0,1,2:T(8,128)(2,1)S(1)}, u32[]{:S(2)}, u32[]{:S(2)}) async-start(bf16[8,1,4,36864]{3,0,1,2:T(8,128)(2,1)} %copy.260), calls=%async_computation.18 | async-start | bytes 4718592 | tf_op jit(solution)/shard_map/all_to_all | solution.py:146
  404.9 19.9 %copy-start.21 = (s32[8,1,32,2]{2,3,1,0:T(2,128)S(1)}, s32[8,1,32,2]{2,3,1,0:T(2,128)}, u32[]{:S(2)}) copy-start(s32[8,1,32,2]{2,3,1,0:T(2,128)} %copy-done.20) | copy-start | bytes 6148
  418.1 1.5 copy-start.4
  419.5 59.5 %all-to-all-start.10 = ((bf16[8,1,4,36864]{3,0,1,2:T(8,128)(2,1)}), bf16[8,1,4,36864]{3,0,1,2:T(8,128)(2,1)}, u32[]{:S(2)}, u32[]{:S(2)}) async-start(bf16[8,1,4,36864]{3,0,1,2:T(8,128)(2,1)} %copy.242), calls=%async_computation.10 | async-start | bytes 4718592 | tf_op jit(solution)/shard_map/all_to_all | solution.py:145
  470.9 4.3 copy-start.6
  470.9 4.4 copy-start.27
  479.0 42.9 %copy-start.5 = (bf16[8,1,4,36864]{3,0,1,2:T(8,128)(2,1)S(1)}, bf16[8,1,4,36864]{3,0,1,2:T(8,128)(2,1)}, u32[]{:S(2)}) copy-start(bf16[8,1,4,36864]{3,0,1,2:T(8,128)(2,1)} %copy-done.4) | copy-start | bytes 7077892
  512.2 62.1 %all-to-all-start.5 = ((bf16[8,1,32,2304]{3,2,1,0:T(8,128)(2,1)}), bf16[8,1,32,2304]{3,2,1,0:T(8,128)(2,1)S(1)}, u32[]{:S(2)}, u32[]{:S(2)}) async-start(bf16[8,1,32,2304]{3,2,1,0:T(8,128)(2,1)} %get-tuple-element.5), calls=%async_computation.5 | async-start | bytes 2359296 | tf_op jit(solution)/shard_map/all_to_all | solution.py:166
  565.9 4.4 copy-start.7
  565.9 4.4 copy-start.28
  565.9 4.4 copy-start.29
  574.4 38.4 %copy-start.24 = (s32[1,64,4]{1,2,0:T(4,128)S(1)}, s32[1,64,4]{1,2,0:T(4,128)}, u32[]{:S(2)}) copy-start(s32[1,64,4]{1,2,0:T(4,128)} %copy-done.23) | copy-start | bytes 3076
  574.4 39.2 %copy-start.26 = (s32[1,64,4]{1,2,0:T(4,128)S(1)}, s32[1,64,4]{1,2,0:T(4,128)}, u32[]{:S(2)}) copy-start(s32[1,64,4]{1,2,0:T(4,128)} %copy-done.25) | copy-start | bytes 3076
  574.4 41.6 %copy-start.2 = (bf16[8,1,32,2304]{3,2,1,0:T(8,128)(2,1)S(1)}, bf16[8,1,32,2304]{3,2,1,0:T(8,128)(2,1)}, u32[]{:S(2)}) copy-start(bf16[8,1,32,2304]{3,2,1,0:T(8,128)(2,1)} %all_to_all.100) | copy-start | bytes 3538948
  608.3 32.9 %all-to-all-start.19 = ((bf16[8,1,32,2304]{3,2,1,0:T(8,128)(2,1)}), bf16[8,1,32,2304]{3,2,1,0:T(8,128)(2,1)S(1)}, u32[]{:S(2)}, u32[]{:S(2)}) async-start(bf16[8,1,32,2304]{3,2,1,0:T(8,128)(2,1)} %get-tuple-element.6), calls=%async_computation.19 | async-start | bytes 2359296 | tf_op jit(solution)/shard_map/all_to_all | solution.py:167
  623.7 2.9 copy-start.3
  642.6 1.8 copy-start.13
  642.7 1.8 copy-start.31
  642.7 1.8 copy-start.32
  644.5 4.5 copy-start.1
where the time goes:
time: 661 us; the launch traced here: 649 us
  local copies, waits for them, and re-layouts  254 us (38%)
  waiting for transfers between devices  158 us (24%)
  starting transfers between devices  82.4 us (12%)
  matrix products  67.2 us (10%)
  blocking collectives  67.1 us (10%)
  other arithmetic  19.1 us (3%)
    all_to_all x2, waiting for transfers between devices, micro_run(): lax.all_to_all(send_tokens, 'grp', split_axis=0, concat_axis=0, tiled=True)  51.8 us
    gather x8, local copies, waits for them, and re-layouts, take_rows(): return table[indices]  50 us
    all_to_all x2, waiting for transfers between devices, micro_run(): lax.all_to_all(send_cotan, 'grp', split_axis=0, concat_axis=0, tiled=True)  38.8 us
    all_to_all x1, blocking collectives, micro_run(): lax.all_to_all(pair_out, 'grp', split_axis=0, concat_axis=0, tiled=True)  33.9 us
    reshape x8, local copies, waits for them, and re-layouts, apply_blocks(): return (out_rows.reshape(dims_shape), grad_rows.reshape(dims_shape))  33.5 us
    all_to_all x1, blocking collectives, micro_run(): lax.all_to_all(pair_grad, 'grp', split_axis=0, concat_axis=0, tiled=True)  33.2 us
    reshape x4, local copies, waits for them, and re-layouts, micro_run(): place_tokens.astype(jnp.bfloat16)  18.2 us
    reshape x4, local copies, waits for them, and re-layouts, micro_run(): place_cotan.astype(jnp.bfloat16)  18.1 us
  transfers between devices with their start and end apart: 18, of which 13 were waited for; matrix products, arithmetic and copies ran while one was open for 49% of the time, Pallas kernels for 0%

commit v1 on v0

v1 whole, which is shorter than its diff:
```python
import functools

import jax
import jax.numpy as jnp
from jax import lax
from jax.experimental import pallas as pl
from jax.experimental.pallas import tpu as pltpu
from jax.sharding import PartitionSpec as P

PAIR = 2
LAG_EXPERT = 1
LAG_RETURN = 2
MESH = pl.DeviceIdType.MESH
TRANS_RHS = (((1,), (1,)), ((), ()))


def xor(a, b, size):
    out = 0
    bit = 1
    while bit < size:
        out = out + ((a // bit + b // bit) % 2) * bit
        bit *= 2
    return out


def order_of(i, groups):
    if groups <= 4:
        return i
    late = (i + groups - 2) // groups
    return (1 - late) * i + late * (2 + i % (groups - 2))


def moe_kernel(
    groups,
    peers,
    joined,
    tok_ref,
    cot_ref,
    pick_ref,
    slot_ref,
    sum_ref,
    gate_hbm,
    up_hbm,
    down_hbm,
    out_ref,
    grad_ref,
    gate_ref,
    up_ref,
    down_ref,
    zsend,
    zrecv,
    zback,
    xysend,
    xyrecv,
    xyback,
    w_sem,
    zs_sem,
    zr_sem,
    bs_sem,
    br_sem,
    ds_sem,
    dr_sem,
    rs_sem,
    rr_sem,
):
    g = lax.axis_index("grp")
    l = lax.axis_index("dev")
    width = tok_ref.shape[1]
    wide = 2 * width
    chunks = groups // joined
    group_rows = zrecv.shape[1]
    slots = slot_ref.shape[2]
    peer_rows = slots // peers

    barrier = pltpu.get_barrier_semaphore()
    for k in range(1, groups):
        pl.semaphore_signal(
            barrier, inc=1, device_id={"grp": xor(g, k, groups)}, device_id_type=MESH
        )
    for q in range(1, peers):
        pl.semaphore_signal(
            barrier, inc=1, device_id={"dev": xor(l, q, peers)}, device_id_type=MESH
        )

    loads = [
        pltpu.make_async_copy(src, dst, w_sem.at[n])
        for n, (src, dst) in enumerate(
            ((gate_hbm, gate_ref), (up_hbm, up_ref), (down_hbm, down_ref))
        )
    ]
    for load in loads:
        load.start()

    def z_copy(i):
        return pltpu.make_async_remote_copy(
            src_ref=zsend.at[i],
            dst_ref=zrecv.at[i],
            send_sem=zs_sem.at[i],
            recv_sem=zr_sem.at[i],
            device_id={"grp": xor(g, order_of(i, groups), groups)},
            device_id_type=MESH,
        )

    def z_back(i):
        return pltpu.make_async_remote_copy(
            src_ref=zrecv.at[i, :, pl.ds(0, wide)],
            dst_ref=zback.at[i],
            send_sem=bs_sem.at[i],
            recv_sem=br_sem.at[i],
            device_id={"grp": xor(g, order_of(i, groups), groups)},
            device_id_type=MESH,
        )

    def xy_copy(c, q):
        return pltpu.make_async_remote_copy(
            src_ref=xysend.at[c, q],
            dst_ref=xyrecv.at[c, q],
            send_sem=ds_sem.at[c, q],
            recv_sem=dr_sem.at[c, q],
            device_id={"dev": xor(l, q, peers)},
            device_id_type=MESH,
        )

    def xy_back(c, q):
        return pltpu.make_async_remote_copy(
            src_ref=xyrecv.at[c, q],
            dst_ref=xyback.at[c, q],
            send_sem=rs_sem.at[c, q],
            recv_sem=rr_sem.at[c, q],
            device_id={"dev": xor(l, q, peers)},
            device_id_type=MESH,
        )

    def fill(i, target):
        pick = pick_ref[i]
        for source, low in ((tok_ref, 0), (cot_ref, width)):
            target[i, :, low : low + width] = jnp.dot(
                pick, source[...], preferred_element_type=jnp.float32
            ).astype(jnp.bfloat16)
        target[i, :, wide : wide + slots] = jnp.dot(
            pick, slot_ref[i], preferred_element_type=jnp.float32
        ).astype(jnp.bfloat16)

    fill(0, zrecv)

    def fill_step(i, carry):
        fill(i, zsend)
        return carry

    lax.fori_loop(1, groups, fill_step, 0)
    pl.semaphore_wait(barrier, groups + peers - 2)

    def send_step(i, carry):
        z_copy(i).start()
        return carry

    lax.fori_loop(1, groups, send_step, 0)

    def chunk_weights(c):
        block = zrecv[pl.ds(c * joined, joined), :, wide : wide + slots]
        return block.reshape(joined * group_rows, slots)

    def place(c):
        for j in range(joined):
            i = c * joined + j

            @pl.when(i > 0)
            def _():
                z_copy(i).wait_recv()

        weights = chunk_weights(c).astype(jnp.float32)
        select = jnp.where(weights != 0.0, 1.0, 0.0).T.astype(jnp.bfloat16)
        rows = zrecv[pl.ds(c * joined, joined), :, 0:wide].reshape(joined * group_rows, wide)
        placed = jnp.dot(select, rows, preferred_element_type=jnp.float32).astype(jnp.bfloat16)
        for q in range(1, peers):
            xysend[c, q] = placed[q * peer_rows : (q + 1) * peer_rows]
            xy_copy(c, q).start()
        xyrecv[c, 0] = placed[0:peer_rows]

    def expert(c):
        @pl.when(c == 0)
        def _():
            for load in loads:
                load.wait()

        for q in range(1, peers):
            xy_copy(c, q).wait_recv()
        rows_x = xyrecv[c, :, :, 0:width].reshape(slots, width)
        rows_dy = xyrecv[c, :, :, width:wide].reshape(slots, width)
        gate_pre = jnp.dot(rows_x, gate_ref[...], preferred_element_type=jnp.float32)
        up_pre = jnp.dot(rows_x, up_ref[...], preferred_element_type=jnp.float32)
        act_grad = lax.dot_general(
            rows_dy, down_ref[...], TRANS_RHS, preferred_element_type=jnp.float32
        )
        sig = jax.nn.sigmoid(gate_pre)
        gate_act = gate_pre * sig
        act = (gate_act * up_pre).astype(jnp.bfloat16)
        gate_grad = (act_grad * up_pre * sig * (1.0 + gate_pre * (1.0 - sig))).astype(jnp.bfloat16)
        up_grad = (act_grad * gate_act).astype(jnp.bfloat16)
        expert_out = jnp.dot(act, down_ref[...], preferred_element_type=jnp.float32)
        xyrecv[c, :, :, 0:width] = expert_out.astype(jnp.bfloat16).reshape(peers, peer_rows, width)
        expert_grad = lax.dot_general(
            gate_grad, gate_ref[...], TRANS_RHS, preferred_element_type=jnp.float32
        ) + lax.dot_general(up_grad, up_ref[...], TRANS_RHS, preferred_element_type=jnp.float32)
        xyrecv[c, :, :, width:wide] = expert_grad.astype(jnp.bfloat16).reshape(
            peers, peer_rows, width
        )
        for q in range(1, peers):
            xy_back(c, q).start()
        xyback[c, 0] = xyrecv[c, 0]

    def combine(c):
        for q in range(1, peers):
            xy_back(c, q).wait_recv()
        weights = chunk_weights(c)
        pairs = jnp.dot(
            weights, xyback[c].reshape(slots, wide), preferred_element_type=jnp.float32
        ).astype(jnp.bfloat16)
        zrecv[pl.ds(c * joined, joined), :, 0:wide] = pairs.reshape(joined, group_rows, wide)
        for j in range(joined):
            i = c * joined + j

            @pl.when(i > 0)
            def _():
                z_back(i).start()

    def step(t, carry):
        @pl.when(t < chunks)
        def _():
            place(t)

        @pl.when((t >= LAG_EXPERT) & (t < chunks + LAG_EXPERT))
        def _():
            expert(t - LAG_EXPERT)

        @pl.when(t >= LAG_RETURN)
        def _():
            combine(t - LAG_RETURN)

        return carry

    lax.fori_loop(0, chunks + LAG_RETURN, step, 0)

    zback[0] = zrecv[0, :, 0:wide]

    def finish_step(i, carry):
        z_back(i).wait_recv()
        return carry

    lax.fori_loop(1, groups, finish_step, 0)
    for target, low in ((out_ref, 0), (grad_ref, width)):
        target[...] = jnp.dot(
            sum_ref[...],
            zback[:, :, low : low + width].reshape(groups * group_rows, width),
            preferred_element_type=jnp.float32,
        ).astype(jnp.bfloat16)

    def drain_z(i, carry):
        z_copy(i).wait_send()
        z_back(i).wait_send()
        return carry

    lax.fori_loop(1, groups, drain_z, 0)

    def drain_xy(c, carry):
        for q in range(1, peers):
            xy_copy(c, q).wait_send()
            xy_back(c, q).wait_send()
        return carry

    lax.fori_loop(0, chunks, drain_xy, 0)


def routing(expert_ids, combine_weights, live_counts, groups, peers, joined):
    rows, top_count = expert_ids.shape
    micro_count = live_counts.shape[1]
    rows_mb = rows // micro_count
    experts = groups * peers
    per_expert = rows * top_count // experts
    per_group = per_expert * peers // PAIR
    g = lax.axis_index("grp")
    l = lax.axis_index("dev")
    relative = ((expert_ids // peers) ^ g) * peers + ((expert_ids % peers) ^ l)
    order = jnp.array([order_of(i, groups) for i in range(groups)], jnp.int32)
    wanted = (order[:, None] * peers + jnp.arange(peers, dtype=jnp.int32)).reshape(-1)
    hit = relative[:, :, None] == wanted
    member = jnp.any(hit, axis=1)
    weight = jnp.sum(
        jnp.where(hit, combine_weights.astype(jnp.float32)[:, :, None], 0.0), axis=1
    )
    index = jnp.arange(rows, dtype=jnp.int32)
    live = (index % rows_mb) < jnp.repeat(live_counts[0], rows_mb)
    weight = jnp.where(live[:, None], weight, 0.0).astype(jnp.bfloat16)
    in_group = jnp.any(member.reshape(rows, groups, peers), axis=2)
    both = jnp.concatenate([member, in_group], axis=1).astype(jnp.bfloat16)
    before = (index[:, None] > index[None, :]).astype(jnp.bfloat16)
    rank = jnp.dot(before, both, preferred_element_type=jnp.float32).astype(jnp.int32)
    expert_rank, group_rank = rank[:, :experts], rank[:, experts:]
    group_slot = jnp.where(in_group, group_rank, -1)
    pick = (
        group_slot.T[:, None, :] == jnp.arange(per_group, dtype=jnp.int32)[None, :, None]
    ).astype(jnp.bfloat16)
    total = (
        group_slot[:, :, None] == jnp.arange(per_group, dtype=jnp.int32)
    ).astype(jnp.bfloat16).reshape(rows, groups * per_group)
    offset = (jnp.arange(groups, dtype=jnp.int32) % joined) * per_expert
    expert_slot = expert_rank.reshape(rows, groups, peers) + offset[None, :, None]
    expert_slot = expert_slot.transpose(1, 0, 2)[..., None]
    width = joined * per_expert
    slot = jnp.where(
        expert_slot == jnp.arange(width, dtype=jnp.int32),
        weight.reshape(rows, groups, peers).transpose(1, 0, 2)[..., None],
        jnp.zeros((), jnp.bfloat16),
    ).reshape(groups, rows, peers * width)
    return pick, slot, total


def local(
    tokens, cotangent, expert_ids, combine_weights, live_counts, gate_weight, up_weight, down_weight
):
    groups = lax.axis_size("grp")
    peers = lax.axis_size("dev")
    rows, width = tokens.shape
    hidden = gate_weight.shape[2]
    per_expert = rows * expert_ids.shape[1] // (groups * peers)
    per_group = per_expert * peers // PAIR
    joined = max(1, 16 // per_expert)
    chunks = groups // joined
    peer_rows = joined * per_expert
    slots = peers * peer_rows
    wide = 2 * width
    pick, slot, total = routing(
        expert_ids, combine_weights, live_counts, groups, peers, joined
    )
    vmem = pl.BlockSpec(memory_space=pltpu.VMEM)
    anywhere = pl.BlockSpec(memory_space=pl.ANY)
    dma = pltpu.SemaphoreType.DMA
    bf16 = jnp.bfloat16
    return pl.pallas_call(
        functools.partial(moe_kernel, groups, peers, joined),
        out_shape=(
            jax.ShapeDtypeStruct((rows, width), bf16),
            jax.ShapeDtypeStruct((rows, width), bf16),
        ),
        in_specs=[vmem] * 5 + [anywhere] * 3,
        out_specs=(vmem, vmem),
        scratch_shapes=[
            pltpu.VMEM((width, hidden), bf16),
            pltpu.VMEM((width, hidden), bf16),
            pltpu.VMEM((hidden, width), bf16),
            pltpu.VMEM((groups, per_group, wide + slots), bf16),
            pltpu.VMEM((groups, per_group, wide + slots), bf16),
            pltpu.VMEM((groups, per_group, wide), bf16),
            pltpu.VMEM((chunks, peers, peer_rows, wide), bf16),
            pltpu.VMEM((chunks, peers, peer_rows, wide), bf16),
            pltpu.VMEM((chunks, peers, peer_rows, wide), bf16),
            dma((3,)),
            dma((groups,)),
            dma((groups,)),
            dma((groups,)),
            dma((groups,)),
            dma((chunks, peers)),
            dma((chunks, peers)),
            dma((chunks, peers)),
            dma((chunks, peers)),
        ],
        compiler_params=pltpu.CompilerParams(
            collective_id=0, has_side_effects=True, vmem_limit_bytes=65 * 1024 * 1000
        ),
    )(
        tokens,
        cotangent,
        pick,
        slot,
        total,
        gate_weight[0],
        up_weight[0],
        down_weight[0],
    )


def solution(mesh):
    spec2 = P(("grp", "dev"), None)
    spec3 = P(("grp", "dev"), None, None)
    return jax.shard_map(
        local,
        mesh=mesh,
        in_specs=(spec2,) * 5 + (spec3,) * 3,
        out_specs=(spec2, spec2),
        check_vma=False,
    )
```

time: 661 us -> 267 us (0.40); the launches traced: 649 us -> 263 us
  Pallas kernels: 0 us -> 252 us
  local copies, waits for them, and re-layouts: 254 us -> 5.5 us
  waiting for transfers between devices: 158 us -> 0 us
  starting transfers between devices: 82.4 us -> 0 us
  blocking collectives: 67.1 us -> 0 us
  matrix products: 67.2 us -> 0.14 us
  other arithmetic: 19.1 us -> 4.47 us
    pallas_call x0 -> x1, Pallas kernels: none -> 252 us  [local(): pl.pallas_call(functools.partial(moe_kernel, groups, peers, joined), out_...]
    all_to_all x18 -> x0, waiting for transfers between devices: 158 us -> none  [the longest x2 51.8 us: micro_run(): lax.all_to_all(send_tokens, 'grp', split_axis=0, concat_axis=0, tiled=True)]
    reshape x42 -> x1, local copies, waits for them, and re-layouts: 134 us -> 0.08 us  [routing(): live = index % rows_mb < jnp.repeat(live_counts[0], rows_mb)]
    all_to_all x18 -> x0, starting transfers between devices: 82.4 us -> none  [the longest x2 11.5 us: micro_run(): lax.all_to_all(row_weight, 'grp', split_axis=0, concat_axis=0, tiled=True)]
    gather x32 -> x0, local copies, waits for them, and re-layouts: 70.5 us -> none  [the longest x8 50 us: take_rows(): return table[indices]]
    all_to_all x2 -> x0, blocking collectives: 67.1 us -> none  [the longest x1 33.9 us: micro_run(): lax.all_to_all(pair_out, 'grp', split_axis=0, concat_axis=0, tiled=True)]
    dot_general x24 -> x1, matrix products: 67.2 us -> 0.14 us  [routing(): jnp.dot(before, both, preferred_element_type=jnp.float32).astype(jnp.int32)]
    all_to_all x8 -> x0, local copies, waits for them, and re-layouts: 37.6 us -> none  [the longest x2 9.85 us: micro_run(): lax.all_to_all(results[0], 'dev', split_axis=2, concat_axis=2, tiled=True)]
  transfers between devices with their start and end apart: 18 -> 0, of which waited for: 13 -> 0; matrix products, arithmetic and copies ran while one was open for 49% -> 0% of each run, Pallas kernels for 0% -> 0%
where the time goes in v1:
time: 267 us; the launch traced here: 263 us
  Pallas kernels  252 us (94%)
  local copies, waits for them, and re-layouts  5.5 us (2%)
  other arithmetic  4.47 us (2%)
    pallas_call x1, Pallas kernels, local(): pl.pallas_call(functools.partial(moe_kernel, groups, peers, joined), out_...  252 us

profile of v1, /device:TPU:1, one launch (start us, length us, event | category | flops | bytes accessed | tf_op | source)
XLA Modules:
  0.0 262.9 jit_solution(4375256958732322267)
XLA Ops:
  0.6 0.7 broadcast_in_dim.58
  1.4 0.1 reshape.65
  1.5 0.1 eq.81
  1.5 0.7 fusion.8
  2.2 0.7 convert_element_type.21
  2.9 0.7 iota_add_fusion
  3.7 0.1 add.53
  3.7 0.1 compare_reduce_fusion
  3.8 0.1 fusion.1
  4.0 0.1 eq.87
  4.0 0.1 convolution_convert_fusion
  4.2 0.7 fusion.pick_ref
  4.9 0.2 copy.22
  5.2 0.1 copy.23
  5.3 0.7 compare_convert_fusion.sum_ref
  6.0 0.2 copy.21
  6.2 0.8 compare_select_fusion.slot_ref
  7.0 252.1 %shard_map.104 = (bf16[128,2304]{1,0:T(8,128)(2,1)}, bf16[128,2304]{1,0:T(8,128)(2,1)}) custom-call(bf16[128,2304]{1,0:T(8,128)(2,1)} %tok_ref.1, bf16[128,2304]{1,0:T(8,128)(2,1)} %cot_ref.1, bf16[8,64,128]{2,1,0:T(8,128)(2,1)} %fusion.pick_ref, bf16[8,128,128]{2,1,0:T(8,128)(2,1)} %compare_select_fusion.slot_ref, ...), custom_call_target="tpu_custom_call" | custom-call | tf_op jit(solution)/shard_map/pallas_call | solution.py:339
  259.1 1.9 copy.26
  261.0 1.9 copy.27
  (10 shorter events, 0.2 us)

commit v2 on v1

--- a/solution.py
+++ b/solution.py
@@ -23,17 +23,25 @@
     return out
 
 
-def order_of(i, groups):
-    if groups <= 4:
-        return i
-    late = (i + groups - 2) // groups
-    return (1 - late) * i + late * (2 + i % (groups - 2))
+def chunk_order(groups):
+    if groups < 4:
+        return list(range(groups))
+    return [0, 2] + list(range(4, groups)) + [3, 1]
+
+
+def distance_of(unit, parts, groups):
+    i = unit // parts
+    out = 0
+    for k, value in enumerate(chunk_order(groups)):
+        out = out + value * ((i + groups - k) // groups - (i + groups - k - 1) // groups)
+    return out
 
 
 def moe_kernel(
     groups,
     peers,
     joined,
+    parts,
     tok_ref,
     cot_ref,
     pick_ref,
@@ -67,7 +75,8 @@
     l = lax.axis_index("dev")
     width = tok_ref.shape[1]
     wide = 2 * width
-    chunks = groups // joined
+    units = groups * parts
+    chunks = units // joined
     group_rows = zrecv.shape[1]
     slots = slot_ref.shape[2]
     peer_rows = slots // peers
@@ -97,7 +106,7 @@
             dst_ref=zrecv.at[i],
             send_sem=zs_sem.at[i],
             recv_sem=zr_sem.at[i],
-            device_id={"grp": xor(g, order_of(i, groups), groups)},
+            device_id={"grp": xor(g, distance_of(i, parts, groups), groups)},
             device_id_type=MESH,
         )
 
@@ -107,7 +116,7 @@
             dst_ref=zback.at[i],
             send_sem=bs_sem.at[i],
             recv_sem=br_sem.at[i],
-            device_id={"grp": xor(g, order_of(i, groups), groups)},
+            device_id={"grp": xor(g, distance_of(i, parts, groups), groups)},
             device_id_type=MESH,
         )
 
@@ -138,23 +147,24 @@
                 pick, source[...], preferred_element_type=jnp.float32
             ).astype(jnp.bfloat16)
         target[i, :, wide : wide + slots] = jnp.dot(
-            pick, slot_ref[i], preferred_element_type=jnp.float32
+            pick, slot_ref[i // parts], preferred_element_type=jnp.float32
         ).astype(jnp.bfloat16)
 
-    fill(0, zrecv)
+    for i in range(parts):
+        fill(i, zrecv)
 
     def fill_step(i, carry):
         fill(i, zsend)
         return carry
 
-    lax.fori_loop(1, groups, fill_step, 0)
+    lax.fori_loop(parts, units, fill_step, 0)
     pl.semaphore_wait(barrier, groups + peers - 2)
 
     def send_step(i, carry):
         z_copy(i).start()
         return carry
 
-    lax.fori_loop(1, groups, send_step, 0)
+    lax.fori_loop(parts, units, send_step, 0)
 
     def chunk_weights(c):
         block = zrecv[pl.ds(c * joined, joined), :, wide : wide + slots]
@@ -164,7 +174,7 @@
         for j in range(joined):
             i = c * joined + j
 
-            @pl.when(i > 0)
+            @pl.when(i >= parts)
             def _():
                 z_copy(i).wait_recv()
 
@@ -220,7 +230,7 @@
         for j in range(joined):
             i = c * joined + j
 
-            @pl.when(i > 0)
+            @pl.when(i >= parts)
             def _():
                 z_back(i).start()
 
@@ -241,17 +251,18 @@
 
     lax.fori_loop(0, chunks + LAG_RETURN, step, 0)
 
-    zback[0] = zrecv[0, :, 0:wide]
+    for i in range(parts):
+        zback[i] = zrecv[i, :, 0:wide]
 
     def finish_step(i, carry):
         z_back(i).wait_recv()
         return carry
 
-    lax.fori_loop(1, groups, finish_step, 0)
+    lax.fori_loop(parts, units, finish_step, 0)
     for target, low in ((out_ref, 0), (grad_ref, width)):
         target[...] = jnp.dot(
             sum_ref[...],
-            zback[:, :, low : low + width].reshape(groups * group_rows, width),
+            zback[:, :, low : low + width].reshape(units * group_rows, width),
             preferred_element_type=jnp.float32,
         ).astype(jnp.bfloat16)
 
@@ -260,7 +271,7 @@
         z_back(i).wait_send()
         return carry
 
-    lax.fori_loop(1, groups, drain_z, 0)
+    lax.fori_loop(parts, units, drain_z, 0)
 
     def drain_xy(c, carry):
         for q in range(1, peers):
@@ -273,15 +284,16 @@
 
 def routing(expert_ids, combine_weights, live_counts, groups, peers, joined):
     rows, top_count = expert_ids.shape
-    micro_count = live_counts.shape[1]
-    rows_mb = rows // micro_count
+    parts = live_counts.shape[1]
+    rows_mb = rows // parts
     experts = groups * peers
-    per_expert = rows * top_count // experts
+    units = groups * parts
+    per_expert = rows_mb * top_count // experts
     per_group = per_expert * peers // PAIR
     g = lax.axis_index("grp")
     l = lax.axis_index("dev")
     relative = ((expert_ids // peers) ^ g) * peers + ((expert_ids % peers) ^ l)
-    order = jnp.array([order_of(i, groups) for i in range(groups)], jnp.int32)
+    order = jnp.array(chunk_order(groups), jnp.int32)
     wanted = (order[:, None] * peers + jnp.arange(peers, dtype=jnp.int32)).reshape(-1)
     hit = relative[:, :, None] == wanted
     member = jnp.any(hit, axis=1)
@@ -289,24 +301,34 @@
         jnp.where(hit, combine_weights.astype(jnp.float32)[:, :, None], 0.0), axis=1
     )
     index = jnp.arange(rows, dtype=jnp.int32)
+    part = index // rows_mb
     live = (index % rows_mb) < jnp.repeat(live_counts[0], rows_mb)
     weight = jnp.where(live[:, None], weight, 0.0).astype(jnp.bfloat16)
     in_group = jnp.any(member.reshape(rows, groups, peers), axis=2)
     both = jnp.concatenate([member, in_group], axis=1).astype(jnp.bfloat16)
-    before = (index[:, None] > index[None, :]).astype(jnp.bfloat16)
+    before = (
+        (index[:, None] > index[None, :]) & (part[:, None] == part[None, :])
+    ).astype(jnp.bfloat16)
     rank = jnp.dot(before, both, preferred_element_type=jnp.float32).astype(jnp.int32)
     expert_rank, group_rank = rank[:, :experts], rank[:, experts:]
-    group_slot = jnp.where(in_group, group_rank, -1)
+    group_slot = jnp.where(in_group, group_rank + part[:, None] * per_group, -1)
+    unit_rows = jnp.arange(parts * per_group, dtype=jnp.int32)
     pick = (
-        group_slot.T[:, None, :] == jnp.arange(per_group, dtype=jnp.int32)[None, :, None]
-    ).astype(jnp.bfloat16)
+        (group_slot.T[:, None, :] == unit_rows[None, :, None])
+        .astype(jnp.bfloat16)
+        .reshape(units, per_group, rows)
+    )
     total = (
-        group_slot[:, :, None] == jnp.arange(per_group, dtype=jnp.int32)
-    ).astype(jnp.bfloat16).reshape(rows, groups * per_group)
-    offset = (jnp.arange(groups, dtype=jnp.int32) % joined) * per_expert
-    expert_slot = expert_rank.reshape(rows, groups, peers) + offset[None, :, None]
+        (group_slot[:, :, None] == unit_rows)
+        .astype(jnp.bfloat16)
+        .reshape(rows, units * per_group)
+    )
+    width = joined * per_expert
+    offset = jnp.arange(groups, dtype=jnp.int32)[None, :] * parts + part[:, None]
+    expert_slot = expert_rank.reshape(rows, groups, peers) + (
+        offset % joined * per_expert
+    )[..., None]
     expert_slot = expert_slot.transpose(1, 0, 2)[..., None]
-    width = joined * per_expert
     slot = jnp.where(
         expert_slot == jnp.arange(width, dtype=jnp.int32),
         weight.reshape(rows, groups, peers).transpose(1, 0, 2)[..., None],
@@ -322,10 +344,12 @@
     peers = lax.axis_size("dev")
     rows, width = tokens.shape
     hidden = gate_weight.shape[2]
-    per_expert = rows * expert_ids.shape[1] // (groups * peers)
+    parts = live_counts.shape[1]
+    units = groups * parts
+    per_expert = rows // parts * expert_ids.shape[1] // (groups * peers)
     per_group = per_expert * peers // PAIR
     joined = max(1, 16 // per_expert)
-    chunks = groups // joined
+    chunks = units // joined
     peer_rows = joined * per_expert
     slots = peers * peer_rows
     wide = 2 * width
@@ -337,7 +361,7 @@
     dma = pltpu.SemaphoreType.DMA
     bf16 = jnp.bfloat16
     return pl.pallas_call(
-        functools.partial(moe_kernel, groups, peers, joined),
+        functools.partial(moe_kernel, groups, peers, joined, parts),
         out_shape=(
             jax.ShapeDtypeStruct((rows, width), bf16),
             jax.ShapeDtypeStruct((rows, width), bf16),
@@ -348,17 +372,17 @@
             pltpu.VMEM((width, hidden), bf16),
             pltpu.VMEM((width, hidden), bf16),
             pltpu.VMEM((hidden, width), bf16),
-            pltpu.VMEM((groups, per_group, wide + slots), bf16),
-            pltpu.VMEM((groups, per_group, wide + slots), bf16),
-            pltpu.VMEM((groups, per_group, wide), bf16),
+            pltpu.VMEM((units, per_group, wide + slots), bf16),
+            pltpu.VMEM((units, per_group, wide + slots), bf16),
+            pltpu.VMEM((units, per_group, wide), bf16),
             pltpu.VMEM((chunks, peers, peer_rows, wide), bf16),
             pltpu.VMEM((chunks, peers, peer_rows, wide), bf16),
             pltpu.VMEM((chunks, peers, peer_rows, wide), bf16),
             dma((3,)),
-            dma((groups,)),
-            dma((groups,)),
-            dma((groups,)),
-            dma((groups,)),
+            dma((units,)),
+            dma((units,)),
+            dma((units,)),
+            dma((units,)),
             dma((chunks, peers)),
             dma((chunks, peers)),
             dma((chunks, peers)),

time: 267 us -> 238 us (0.89)
  Pallas kernels: 252 us -> 225 us
    pallas_call x1, Pallas kernels: 252 us -> 225 us  [local(): pl.pallas_call(functools.partial(moe_kernel, groups, peers, joined, parts...]
where the time goes in v2:
time: 238 us; the launch traced here: 236 us
  Pallas kernels  225 us (95%)
  local copies, waits for them, and re-layouts  5.46 us (2%)
  other arithmetic  4.6 us (2%)
    pallas_call x1, Pallas kernels, local(): pl.pallas_call(functools.partial(moe_kernel, groups, peers, joined, parts...  225 us

profile of v2, /device:TPU:1, one launch (start us, length us, event | category | flops | bytes accessed | tf_op | source)
XLA Modules:
  0.0 236.0 jit_solution(10384257131012733923)
XLA Ops:
  0.7 0.7 broadcast_in_dim.38
  1.4 0.1 reshape.115
  1.5 0.1 eq.118
  1.6 0.7 fusion.12
  2.3 0.7 convert_element_type.22
  3.0 0.7 iota_add_fusion
  3.7 0.1 add.82
  3.8 0.1 compare_reduce_fusion
  3.9 0.1 fusion
  4.0 0.1 eq.124
  4.1 0.2 convolution_convert_fusion
  4.3 0.8 compare_convert_fusion.1.pick_ref
  5.2 0.2 copy.22
  5.4 0.2 copy.21
  5.6 0.8 compare_select_fusion.slot_ref
  6.4 0.1 copy.23
  6.5 0.7 compare_convert_fusion.sum_ref
  7.2 225.0 %shard_map.104 = (bf16[128,2304]{1,0:T(8,128)(2,1)}, bf16[128,2304]{1,0:T(8,128)(2,1)}) custom-call(bf16[128,2304]{1,0:T(8,128)(2,1)} %tok_ref.1, bf16[128,2304]{1,0:T(8,128)(2,1)} %cot_ref.1, bf16[16,32,128]{2,1,0:T(8,128)(2,1)} %compare_convert_fusion.1.pick_ref, bf16[8,128,64]{2,1,0:T(8,128)(2,1)} %compare_select_fusion.slot_ref, ...), custom_call_target="tpu_custom_call" | custom-call | tf_op jit(solution)/shard_map/pallas_call | solution.py:363
  232.1 1.9 copy.26
  234.1 1.9 copy.27
  (15 shorter events, 0.2 us)

commit v3 on v2

--- a/solution.py
+++ b/solution.py
@@ -24,9 +24,9 @@
 
 
 def chunk_order(groups):
-    if groups < 4:
+    if groups < 8:
         return list(range(groups))
-    return [0, 2] + list(range(4, groups)) + [3, 1]
+    return [0, 4, 2] + list(range(5, groups)) + [3, 1]
 
 
 def distance_of(unit, parts, groups):
@@ -153,19 +153,6 @@
     for i in range(parts):
         fill(i, zrecv)
 
-    def fill_step(i, carry):
-        fill(i, zsend)
-        return carry
-
-    lax.fori_loop(parts, units, fill_step, 0)
-    pl.semaphore_wait(barrier, groups + peers - 2)
-
-    def send_step(i, carry):
-        z_copy(i).start()
-        return carry
-
-    lax.fori_loop(parts, units, send_step, 0)
-
     def chunk_weights(c):
         block = zrecv[pl.ds(c * joined, joined), :, wide : wide + slots]
         return block.reshape(joined * group_rows, slots)
@@ -175,7 +162,7 @@
             i = c * joined + j
 
             @pl.when(i >= parts)
-            def _():
+            def _(i=i):
                 z_copy(i).wait_recv()
 
         weights = chunk_weights(c).astype(jnp.float32)
@@ -234,8 +221,22 @@
             def _():
                 z_back(i).start()
 
+    early = min(1, parts // joined)
+    pl.semaphore_wait(barrier, groups + peers - 2)
+    for c in range(early):
+        place(c)
+    fill(parts, zsend)
+
+    def send_step(i, carry):
+        fill(i, zsend)
+        z_copy(i - 1).start()
+        return carry
+
+    lax.fori_loop(parts + 1, units, send_step, 0)
+    z_copy(units - 1).start()
+
     def step(t, carry):
-        @pl.when(t < chunks)
+        @pl.when((t >= early) & (t < chunks))
         def _():
             place(t)
 

time: 238 us -> 235 us (0.987)
  no operation moved by 1% of the time
where the time goes in v3:
time: 235 us
  Pallas kernels  224 us (95%)
  local copies, waits for them, and re-layouts  5.46 us (2%)
  other arithmetic  4.6 us (2%)
    pallas_call x1, Pallas kernels, local(): pl.pallas_call(functools.partial(moe_kernel, groups, peers, joined, parts...  224 us

profile of v3, /device:TPU:1, one launch (start us, length us, event | category | flops | bytes accessed | tf_op | source)
XLA Modules:
  0.0 235.2 jit_solution(11379799778235385655)
XLA Ops:
  0.7 0.7 broadcast_in_dim.38
  1.4 0.1 reshape.115
  1.5 0.1 eq.118
  1.6 0.7 fusion.12
  2.3 0.7 convert_element_type.22
  3.0 0.7 iota_add_fusion
  3.7 0.1 add.82
  3.8 0.1 compare_reduce_fusion
  3.9 0.1 fusion
  4.0 0.1 eq.124
  4.1 0.2 convolution_convert_fusion
  4.3 0.8 compare_convert_fusion.1.pick_ref
  5.2 0.2 copy.22
  5.4 0.2 copy.21
  5.6 0.8 compare_select_fusion.slot_ref
  6.4 0.1 copy.23
  6.5 0.7 compare_convert_fusion.sum_ref
  7.2 224.1 %shard_map.104 = (bf16[128,2304]{1,0:T(8,128)(2,1)}, bf16[128,2304]{1,0:T(8,128)(2,1)}) custom-call(bf16[128,2304]{1,0:T(8,128)(2,1)} %tok_ref.1, bf16[128,2304]{1,0:T(8,128)(2,1)} %cot_ref.1, bf16[16,32,128]{2,1,0:T(8,128)(2,1)} %compare_convert_fusion.1.pick_ref, bf16[8,128,64]{2,1,0:T(8,128)(2,1)} %compare_select_fusion.slot_ref, ...), custom_call_target="tpu_custom_call" | custom-call | tf_op jit(solution)/shard_map/pallas_call | solution.py:364
  231.3 1.9 copy.26
  233.3 1.9 copy.27
  (15 shorter events, 0.2 us)

commit v4 on v3

--- a/solution.py
+++ b/solution.py
@@ -221,7 +221,7 @@
             def _():
                 z_back(i).start()
 
-    early = min(1, parts // joined)
+    early = parts // joined
     pl.semaphore_wait(barrier, groups + peers - 2)
     for c in range(early):
         place(c)

time: 235 us -> 236 us (level)
  no operation moved by 1% of the time
where the time goes in v4:
time: 236 us
  Pallas kernels  225 us (95%)
  local copies, waits for them, and re-layouts  5.46 us (2%)
  other arithmetic  4.6 us (2%)
    pallas_call x1, Pallas kernels, local(): pl.pallas_call(functools.partial(moe_kernel, groups, peers, joined, parts...  225 us

profile of v4, /device:TPU:1, one launch (start us, length us, event | category | flops | bytes accessed | tf_op | source)
XLA Modules:
  0.0 235.6 jit_solution(13257494084789960485)
XLA Ops:
  0.7 0.7 broadcast_in_dim.38
  1.4 0.1 reshape.115
  1.5 0.1 eq.118
  1.6 0.7 fusion.12
  2.3 0.7 convert_element_type.22
  3.0 0.7 iota_add_fusion
  3.7 0.1 add.82
  3.8 0.1 compare_reduce_fusion
  3.9 0.1 fusion
  4.0 0.1 eq.124
  4.1 0.2 convolution_convert_fusion
  4.3 0.8 compare_convert_fusion.1.pick_ref
  5.2 0.2 copy.22
  5.4 0.2 copy.21
  5.6 0.8 compare_select_fusion.slot_ref
  6.4 0.1 copy.23
  6.5 0.7 compare_convert_fusion.sum_ref
  7.2 224.5 %shard_map.104 = (bf16[128,2304]{1,0:T(8,128)(2,1)}, bf16[128,2304]{1,0:T(8,128)(2,1)}) custom-call(bf16[128,2304]{1,0:T(8,128)(2,1)} %tok_ref.1, bf16[128,2304]{1,0:T(8,128)(2,1)} %cot_ref.1, bf16[16,32,128]{2,1,0:T(8,128)(2,1)} %compare_convert_fusion.1.pick_ref, bf16[8,128,64]{2,1,0:T(8,128)(2,1)} %compare_select_fusion.slot_ref, ...), custom_call_target="tpu_custom_call" | custom-call | tf_op jit(solution)/shard_map/pallas_call | solution.py:364
  231.7 1.9 copy.26
  233.6 1.9 copy.27
  (15 shorter events, 0.2 us)
